TPU v7x, 512 devices: a whole 4x8x8 slice. The times are simulated.
512 devices in a mesh: dp: 32 (over z, x), tensor: 16 (over y, core).
Axes of the slice: x: 4, y: 8, z: 8, core: 2. Of those that a mesh axis runs over, the one named last changes fastest.
Arguments:
- tokens: int32 [64, 4], P('dp'), may hold values from 0 to 77823
- embed_table: bfloat16 [77824, 3584], P('dp', 'tensor'), may hold values from -6 to 6
- norm_gain: bfloat16 [3584], P('tensor'), may hold values from 0.099609375 to 1.8984375
- w_query: bfloat16 [3584, 2048], P('tensor'), may hold values from -0.09375 to 0.09375
- w_key_value: bfloat16 [3584, 1024], P('tensor'), may hold values from -0.09375 to 0.09375
- cache_keys: bfloat16 [64, 4, 64, 128], P('dp'), may hold values from -6 to 6
- cache_values: bfloat16 [64, 4, 64, 128], P('dp'), may hold values from -6 to 6
- cache_len: int32 [64], P('dp'), may hold values from 1 to 64, 2048 in all
- teacher_rows: bfloat16 [512, 8192], P('dp', 'tensor'), may hold values from -6 to 6
- w_llama: bfloat16 [8192, 2, 14336], P('tensor', None, 'dp'), may hold values from -0.0625 to 0.0625
- w_qwen: bfloat16 [8192, 2, 14784], P('tensor', None, 'dp'), may hold values from -0.0625 to 0.0625
- rollout_len: int32 [32, 4], P('dp'), may hold values from 1 to 8, 16 in all within a row
- teacher_of: int32 [32, 4], P('dp'), may hold values from 0 to 1
Outputs:
- attn_out: bfloat16 [64, 4, 2048], P('dp', None, 'tensor')
- llama_hidden: bfloat16 [512, 14336], P('tensor', 'dp')
- qwen_hidden: bfloat16 [512, 14784], P('tensor', 'dp')
Inputs may be any that keep to these rules, and one draw needn't show every extreme that they name: `cache_len`: at least one rollout fills all 64 slots. `rollout_len`: each row sums to 16; the longest rollout of a row has 8 token rows.
All inputs are finite; a program needn't handle non-finite values. No bound on the sum of `cache_len` on one device may be relied on, other than what follows from the above.
Results may differ from a plain program's by a relative error of at most 0.01.
Values may be sent and summed in bfloat16 or wider, within the bound.
No kernel may reach another device: no remote copies, remote signals or barrier semaphores. Data moves between devices by JAX's collectives and lax.ppermute only.
A program may use at most 64 MiB of HBM per device.

v0:
```python
import math
import jax
import jax.numpy as jnp
from jax import lax
from jax.sharding import PartitionSpec as P

DS = 3584
HEADS = 16
KVH = 4
HD = 128
TT_DEV = 16


def row_owner(rollout_len, teacher_of, per_group):
    ends = jnp.cumsum(rollout_len, axis=1)
    offset = jnp.arange(per_group, dtype=jnp.int32)
    which = jnp.sum((offset[None, :, None] >= ends[:, None, :]).astype(jnp.int32), axis=2)
    slots = jnp.arange(rollout_len.shape[1], dtype=jnp.int32)
    pick = (which[:, :, None] == slots[None, None, :]).astype(jnp.int32)
    return jnp.sum(pick * teacher_of[:, None, :], axis=2).reshape(-1)


def attend(query, keys_cache, values_cache, keys_new, values_new, cache_len):
    scale = 1.0 / math.sqrt(query.shape[-1])
    query_f = query.astype(jnp.float32)
    score_cache = jnp.einsum("bshd,bhld->bshl", query_f, keys_cache.astype(jnp.float32)) * scale
    score_new = jnp.einsum("bshd,bthd->bsht", query_f, keys_new.astype(jnp.float32)) * scale
    live = jnp.arange(keys_cache.shape[2], dtype=jnp.int32)[None, :] < cache_len[:, None]
    steps = query.shape[1]
    causal = jnp.arange(steps)[:, None] >= jnp.arange(steps)[None, :]
    score_cache = jnp.where(live[:, None, None, :], score_cache, -jnp.inf)
    score_new = jnp.where(causal[None, :, None, :], score_new, -jnp.inf)
    top = jnp.maximum(jnp.max(score_cache, axis=3), jnp.max(score_new, axis=3))[..., None]
    exp_cache = jnp.exp(score_cache - top)
    exp_new = jnp.exp(score_new - top)
    total = jnp.sum(exp_cache, axis=3, keepdims=True) + jnp.sum(exp_new, axis=3, keepdims=True)
    prob_cache = (exp_cache / total).astype(jnp.bfloat16)
    prob_new = (exp_new / total).astype(jnp.bfloat16)
    mixed = jnp.einsum(
        "bshl,bhld->bshd", prob_cache.astype(jnp.float32), values_cache.astype(jnp.float32)
    )
    mixed = mixed + jnp.einsum(
        "bsht,bthd->bshd", prob_new.astype(jnp.float32), values_new.astype(jnp.float32)
    )
    return mixed.astype(jnp.bfloat16)


def shards(
    tokens,
    embed_table,
    norm_gain,
    w_query,
    w_key_value,
    cache_keys,
    cache_values,
    cache_len,
    teacher_rows,
    w_llama,
    w_qwen,
    rollout_len,
    teacher_of,
):
    all_tokens, all_lengths, all_owners = (
        lax.all_gather(tokens, "dp", axis=0, tiled=True),
        lax.all_gather(rollout_len, "dp", axis=0, tiled=True),
        lax.all_gather(teacher_of, "dp", axis=0, tiled=True),
    )
    table_rows = embed_table.shape[0]
    local_id = all_tokens - lax.axis_index("dp") * table_rows
    inside = jnp.logical_and(local_id >= 0, local_id < table_rows)
    picked = jnp.take(embed_table, jnp.clip(local_id, 0, table_rows - 1), axis=0)
    term = jnp.where(inside[:, :, None], picked.astype(jnp.float32), 0.0)
    embedded = lax.psum_scatter(term, "dp", scatter_dimension=0, tiled=True).astype(jnp.bfloat16)
    rollouts, steps, columns = embedded.shape
    x_float = embedded.astype(jnp.float32)
    scaled = (x_float * norm_gain.astype(jnp.float32)).astype(jnp.bfloat16).reshape(-1, columns)
    query_part = jnp.dot(scaled, w_query, preferred_element_type=jnp.float32)
    pair_part = jnp.dot(scaled, w_key_value, preferred_element_type=jnp.float32)
    squares = jnp.sum(x_float * x_float, axis=2).reshape(-1)
    heads_here = HEADS // lax.axis_size("tensor")
    head_first = lax.axis_index("tensor") * heads_here
    query_sum, pair_sum, square_sum = lax.psum((query_part, pair_part, squares), "tensor")
    query_own = lax.dynamic_slice_in_dim(query_sum, head_first * HD, heads_here * HD, 1)
    inverse = lax.rsqrt(square_sum / DS + 1e-06)[:, None]
    query = (query_own * inverse).astype(jnp.bfloat16).reshape(rollouts, steps, heads_here, HD)
    key_value = (pair_sum * inverse).astype(jnp.bfloat16).reshape(rollouts, steps, 2, KVH, HD)
    kv_index = (head_first + jnp.arange(heads_here, dtype=jnp.int32)) // (HEADS // KVH)
    keys_cache = jnp.take(cache_keys, kv_index, axis=1)
    values_cache = jnp.take(cache_values, kv_index, axis=1)
    keys_new = jnp.take(key_value[:, :, 0], kv_index, axis=2)
    values_new = jnp.take(key_value[:, :, 1], kv_index, axis=2)
    attn_out = attend(query, keys_cache, values_cache, keys_new, values_new, cache_len).reshape(
        rollouts, steps, heads_here * HD
    )
    llama_cols = w_llama.shape[2]
    qwen_cols = w_qwen.shape[2]
    llama_flat = w_llama.reshape(w_llama.shape[0], 2 * llama_cols)
    qwen_flat = w_qwen.reshape(w_qwen.shape[0], 2 * qwen_cols)
    piece = lax.all_gather(teacher_rows, "dp", axis=0, tiled=True)
    first_part = jnp.dot(piece, llama_flat, preferred_element_type=jnp.float32)
    second_part = jnp.dot(piece, qwen_flat, preferred_element_type=jnp.float32)
    partial_rows = jnp.concatenate([first_part, second_part], axis=1)
    rows_here = partial_rows.shape[0] // lax.axis_size("tensor")
    row_first = lax.axis_index("tensor") * rows_here
    summed_all = lax.psum(partial_rows, "tensor")
    summed = lax.dynamic_slice_in_dim(summed_all, row_first, rows_here, 0)
    owner_all = row_owner(all_lengths, all_owners, TT_DEV)
    owner = lax.dynamic_slice_in_dim(owner_all, row_first, rows_here, 0)
    gate_llama = summed[:, :llama_cols]
    up_llama = summed[:, llama_cols : 2 * llama_cols]
    gate_qwen = summed[:, 2 * llama_cols : 2 * llama_cols + qwen_cols]
    up_qwen = summed[:, 2 * llama_cols + qwen_cols :]
    llama_hidden = jnp.where((owner == 0)[:, None], jax.nn.silu(gate_llama) * up_llama, 0.0).astype(
        jnp.bfloat16
    )
    qwen_hidden = jnp.where((owner == 1)[:, None], jax.nn.silu(gate_qwen) * up_qwen, 0.0).astype(
        jnp.bfloat16
    )
    return (attn_out, llama_hidden, qwen_hidden)


def solution(mesh):
    return jax.shard_map(
        shards,
        mesh=mesh,
        in_specs=(
            P("dp", None),
            P("dp", "tensor"),
            P("tensor"),
            P("tensor", None),
            P("tensor", None),
            P("dp", None, None, None),
            P("dp", None, None, None),
            P("dp"),
            P("dp", "tensor"),
            P("tensor", None, "dp"),
            P("tensor", None, "dp"),
            P("dp", None),
            P("dp", None),
        ),
        out_specs=(P("dp", None, "tensor"), P("tensor", "dp"), P("tensor", "dp")),
        check_vma=False,
    )
```

profile of v0, /device:TPU:1, one launch (start us, length us, event | category | flops | bytes accessed | tf_op | source)
XLA Modules:
  0.0 396.1 jit_solution(5077311815255898789)
XLA Ops:
  7.2 0.0 copy-start
  7.2 0.0 all-reduce.6.cloned.1.call-start
  7.2 40.1 %all-gather = s32[32,2,4]{2,1,0:T(2,128)S(1)} all-gather(s32[1,2,4]{2,1,0:T(2,128)} %bitcast.99), channel_id=1, replica_groups=mesh['dp'=32,'tensor'=16] {'dp'}, dimensions={0}, use_global_device_ids=true | all-gather | bytes 1056 | tf_op jit(solution)/shard_map/all_gather | solution.py:64
  47.3 0.1 copy.94
  47.4 0.1 copy.97
  47.6 0.0 copy-start.3
  47.6 1.9 copy.98
  49.5 0.1 reshape.298
  49.6 1.2 gather_fusion
  50.8 0.1 copy.110
  51.0 0.2 convert_select_fusion
  51.2 114.2 %all-reduce.7 = bf16[64,4,224]{2,1,0:T(4,128)(2,1)S(1)} all-reduce(f32[64,4,224]{2,1,0:T(4,128)S(1)} %convert_select_fusion), channel_id=2, replica_groups=mesh['dp'=32,'tensor'=16] {'dp'}, use_global_device_ids=true, to_apply=%region_0.2.clone | all-reduce | flops 57344 | bytes 344064
  165.4 1.3 dynamic-slice.14
  167.3 0.1 fusion.23
  167.4 35.3 %all_gather.15 = bf16[512,512]{1,0:T(8,128)(2,1)S(1)} all-gather(bf16[16,512]{1,0:T(8,128)(2,1)S(1)} %copy-done.3), channel_id=1, replica_groups=mesh['dp'=32,'tensor'=16] {'dp'}, dimensions={0}, use_global_device_ids=true | all-gather | bytes 540672 | tf_op jit(solution)/shard_map/all_gather | solution.py:99
  202.7 1.3 copy.105
  204.1 0.2 reshape.181
  204.3 0.7 fusion.53
  205.0 0.0 copy-start.1
  205.0 0.7 fusion.52
  205.6 0.5 copy-done.1
  206.1 0.8 fusion.50
  207.0 2.2 pad_maximum_fusion
  209.2 0.0 all-reduce.6.cloned.1.call-update
  209.3 1.0 copy-done.2
  210.2 0.2 fusion.51
  210.4 0.1 reshape.171
  210.5 92.0 %all-reduce.1 = (f32[8]{0:T(128)S(1)}, f32[8,1024]{1,0:T(8,128)S(1)}) all-reduce(f32[8]{0:T(128)S(1)} %reshape.171, f32[8,1024]{1,0:T(8,128)S(1)} %fusion.51), channel_id=1, replica_groups=mesh['dp'=32,'tensor'=16] {'tensor'}, use_global_device_ids=true, to_apply=%region_3.5 | all-reduce | flops 8200 | bytes 65600 | tf_op jit(solution)/shard_map/psum | solution.py:82
  302.5 31.4 %all-gather.2 = s32[32,1,4]{2,1,0:T(1,128)S(1)} all-gather(s32[1,1,4]{2,1,0:T(1,128)S(1)} %bitcast.100), channel_id=1, replica_groups=mesh['dp'=32,'tensor'=16] {'dp'}, dimensions={0}, use_global_device_ids=true | all-gather | bytes 528 | tf_op jit(solution)/shard_map/all_gather | solution.py:66
  333.9 0.1 copy.103
  334.0 30.2 %all-gather.1 = s32[32,1,4]{2,1,0:T(1,128)S(1)} all-gather(s32[1,1,4]{2,1,0:T(1,128)S(1)} %bitcast.101), channel_id=1, replica_groups=mesh['dp'=32,'tensor'=16] {'dp'}, dimensions={0}, use_global_device_ids=true | all-gather | bytes 528 | tf_op jit(solution)/shard_map/all_gather | solution.py:65
  364.2 0.1 copy.102
  364.4 0.1 copy.104
  364.5 0.1 reshape.179
  364.6 0.1 broadcast_compare_fusion
  364.6 0.1 iota_compare_fusion.3
  364.7 0.1 multiply_convert_fusion
  364.8 16.7 %all-reduce.6.cloned.1.call-done = (f32[8,2048]{1,0:T(8,128)}, f32[512,1820]{0,1:T(8,128)}) async-done(((f32[8,2048]{1,0:T(8,128)}, f32[512,1820]{0,1:T(8,128)}), (f32[8,2048]{1,0:T(8,128)}, f32[512,1820]{0,1:T(8,128)})) %all-reduce.6.cloned.1.call-update) | async-done | bytes 3792912 | tf_op jit(solution)/shard_map/psum | solution.py:82
  381.5 0.8 multiply_convert_fusion.1
  382.3 1.0 fusion.48
  383.2 0.1 fusion.49
  383.4 0.2 fusion.24
  383.6 1.2 fusion.10
  384.8 0.7 copy.107
  385.5 1.3 fusion.8
  386.8 0.7 copy.108
  387.5 0.9 fusion.14
  388.5 0.8 fusion.5
  (29 shorter events, 0.3 us)
Async XLA Ops:
  7.2 197.8 %copy-start = (bf16[512,2,448]{0,2,1:T(8,128)(2,1)S(1)}, bf16[512,2,448]{0,2,1:T(8,128)(2,1)}, u32[]{:S(2)}) copy-start(bf16[512,2,448]{0,2,1:T(8,128)(2,1)} %param.26) | copy-start | bytes 2752516
  7.2 374.3 %all-reduce.6.cloned.1.call-start = ((), (), s32[]{:S(2)}) async-start(), calls=%async_computation | async-start | bytes 7602176 | tf_op jit(solution)/shard_map/psum | solution.py:82
  47.6 117.8 %copy-start.6 = (bf16[224]{0:T(256)(128)(2,1)S(1)}, bf16[224]{0:T(256)(128)(2,1)}, u32[]{:S(2)}) copy-start(bf16[224]{0:T(256)(128)(2,1)} %param.19) | copy-start | bytes 1348
  47.6 119.8 %copy-start.3 = (bf16[16,512]{1,0:T(8,128)(2,1)S(1)}, bf16[16,512]{1,0:T(8,128)(2,1)}, u32[]{:S(2)}) copy-start(bf16[16,512]{1,0:T(8,128)(2,1)} %param.25) | copy-start | bytes 49156
  205.0 1.2 copy-start.1
  209.2 1.0 copy-start.2
  209.2 93.3 %copy-start.4 = (s32[1,4]{1,0:T(1,128)S(1)}, s32[1,4]{1,0:T(1,128)}, u32[]{:S(2)}) copy-start(s32[1,4]{1,0:T(1,128)} %param.29) | copy-start | bytes 52
  209.2 124.8 %copy-start.5 = (s32[1,4]{1,0:T(1,128)S(1)}, s32[1,4]{1,0:T(1,128)}, u32[]{:S(2)}) copy-start(s32[1,4]{1,0:T(1,128)} %param.28) | copy-start | bytes 52
  209.2 155.4 %copy-start.7 = (s32[2]{0:T(128)S(1)}, s32[2]{0:T(128)}, u32[]{:S(2)}) copy-start(s32[2]{0:T(128)} %param.24) | copy-start | bytes 28
Sparse Core Ops, SparseCore 0:
  209.4 172.0 all-reduce.5
where the time goes:
time: 397 us; the launch traced here: 396 us
  blocking collectives  343 us (86%)
  waiting for transfers between devices  16.7 us (4%)
  between operations  14.9 us (4%)
  local copies, waits for them, and re-layouts  9.69 us (2%)
  other arithmetic  6.34 us (2%)
  matrix products  5.2 us (1%)
    unnamed x1, blocking collectives  114 us
    psum x1, blocking collectives, shards(): lax.psum((query_part, pair_part, squares), 'tensor')  92 us
    all_gather x1, blocking collectives, shards(): lax.all_gather(tokens, 'dp', axis=0, tiled=True)  40.1 us
    all_gather x1, blocking collectives, shards(): piece = lax.all_gather(teacher_rows, 'dp', axis=0, tiled=True)  35.3 us
    all_gather x1, blocking collectives, shards(): lax.all_gather(teacher_of, 'dp', axis=0, tiled=True)  31.4 us
    all_gather x1, blocking collectives, shards(): lax.all_gather(rollout_len, 'dp', axis=0, tiled=True)  30.2 us
    psum x1, waiting for transfers between devices, shards(): lax.psum((query_part, pair_part, squares), 'tensor')  16.7 us
  transfers between devices with their start and end apart: 1, of which 1 were waited for; matrix products, arithmetic and copies ran while one was open for 0% of the time, Pallas kernels for 0%

commit v1 on v0

--- a/solution.py
+++ b/solution.py
@@ -61,7 +61,9 @@
     teacher_of,
 ):
     all_tokens, all_lengths, all_owners = (
-        lax.all_gather(tokens, "dp", axis=0, tiled=True),
+        jnp.concatenate(
+            lax.all_to_all(jnp.stack([tokens] * lax.axis_size("dp")), "dp", 0, 0), axis=0
+        ),
         lax.all_gather(rollout_len, "dp", axis=0, tiled=True),
         lax.all_gather(teacher_of, "dp", axis=0, tiled=True),
     )

time: 397 us -> 364 us (0.917)
  blocking collectives: 343 us -> 310 us
  starting transfers between devices: 0.04 us -> 13.7 us
  waiting for transfers between devices: 16.7 us -> 4.23 us
    all_gather x1 -> x0, blocking collectives: 40.1 us -> none  [shards(): lax.all_gather(tokens, 'dp', axis=0, tiled=True)]
    all_to_all x0 -> x1, starting transfers between devices: none -> 13.7 us  [shards(): lax.all_to_all(jnp.stack([tokens] * lax.axis_size('dp')), 'dp', 0, 0)]
    psum x1, waiting for transfers between devices: 16.7 us -> 4.21 us  [shards(): lax.psum((query_part, pair_part, squares), 'tensor')]
    psum x1, blocking collectives: 92 us -> 98.2 us  [shards(): lax.psum((query_part, pair_part, squares), 'tensor')]
  transfers between devices with their start and end apart: 1 -> 2, of which waited for: 1 -> 1; matrix products, arithmetic and copies ran while one was open for 0% -> 2% of each run, Pallas kernels for 0% -> 0%
where the time goes in v1:
time: 364 us
  blocking collectives  310 us (85%)
  between operations  14.9 us (4%)
  starting transfers between devices  13.7 us (4%)
  local copies, waits for them, and re-layouts  9.34 us (3%)
  other arithmetic  6.34 us (2%)
  matrix products  5.21 us (1%)
  waiting for transfers between devices  4.23 us (1%)
    unnamed x1, blocking collectives  114 us
    psum x1, blocking collectives, shards(): lax.psum((query_part, pair_part, squares), 'tensor')  98.2 us
    all_gather x1, blocking collectives, shards(): piece = lax.all_gather(teacher_rows, 'dp', axis=0, tiled=True)  38.6 us
    all_gather x1, blocking collectives, shards(): lax.all_gather(rollout_len, 'dp', axis=0, tiled=True)  29.4 us
    all_gather x1, blocking collectives, shards(): lax.all_gather(teacher_of, 'dp', axis=0, tiled=True)  29.3 us
    all_to_all x1, starting transfers between devices, shards(): lax.all_to_all(jnp.stack([tokens] * lax.axis_size('dp')), 'dp', 0, 0)  13.7 us
  transfers between devices with their start and end apart: 2, of which 1 were waited for; matrix products, arithmetic and copies ran while one was open for 2% of the time, Pallas kernels for 0%

profile of v1, /device:TPU:1, one launch (start us, length us, event | category | flops | bytes accessed | tf_op | source)
XLA Modules:
  0.0 363.5 jit_solution(8620308361183107889)
XLA Ops:
  7.2 0.0 copy-start
  7.2 1.4 stack.2
  8.6 13.7 %all-to-all-start = ((s32[32,2,4]{2,1,0:T(2,128)}), s32[32,2,4]{2,1,0:T(2,128)S(1)}, u32[]{:S(2)}, u32[]{:S(2)}) async-start(s32[32,2,4]{2,1,0:T(2,128)} %stack.2), calls=%async_computation | async-start | bytes 65536 | tf_op jit(solution)/shard_map/all_to_all | solution.py:65
  22.3 0.0 all-reduce.6.cloned.1.call-start
  22.3 38.6 %all_gather.11 = bf16[512,512]{1,0:T(8,128)(2,1)S(1)} all-gather(bf16[16,512]{1,0:T(8,128)(2,1)} %param.25), channel_id=1, replica_groups=mesh['dp'=32,'tensor'=16] {'dp'}, dimensions={0}, use_global_device_ids=true | all-gather | bytes 540672 | tf_op jit(solution)/shard_map/all_gather | solution.py:101
  61.0 1.3 copy.143
  62.3 0.2 reshape.227
  62.5 0.7 fusion.53
  63.2 0.7 fusion.52
  63.9 0.0 copy-start.1
  63.9 2.2 pad_maximum_fusion
  66.1 1.0 copy.136
  67.1 0.0 copy-start.2
  67.2 1.3 dynamic-slice.14
  69.2 0.1 copy.131
  69.3 0.1 copy.134
  69.4 0.1 reshape.344
  69.5 1.2 gather_fusion
  70.7 0.1 copy.148
  70.9 0.2 convert_select_fusion
  71.1 114.3 %all-reduce.7 = bf16[64,4,224]{2,1,0:T(4,128)(2,1)S(1)} all-reduce(f32[64,4,224]{2,1,0:T(4,128)S(1)} %convert_select_fusion), channel_id=2, replica_groups=mesh['dp'=32,'tensor'=16] {'dp'}, use_global_device_ids=true, to_apply=%region_0.2.clone | all-reduce | flops 57344 | bytes 344064
  185.4 0.1 fusion.23
  185.5 0.9 fusion.50
  186.4 0.0 all-reduce.6.cloned.1.call-update
  186.4 0.6 copy-done.4
  187.0 29.3 %all-gather.1 = s32[32,1,4]{2,1,0:T(1,128)S(1)} all-gather(s32[1,1,4]{2,1,0:T(1,128)S(1)} %bitcast.101), channel_id=1, replica_groups=mesh['dp'=32,'tensor'=16] {'dp'}, dimensions={0}, use_global_device_ids=true | all-gather | bytes 528 | tf_op jit(solution)/shard_map/all_gather | solution.py:68
  216.3 0.1 copy.141
  216.4 29.4 %all-gather = s32[32,1,4]{2,1,0:T(1,128)S(1)} all-gather(s32[1,1,4]{2,1,0:T(1,128)S(1)} %bitcast.102), channel_id=1, replica_groups=mesh['dp'=32,'tensor'=16] {'dp'}, dimensions={0}, use_global_device_ids=true | all-gather | bytes 528 | tf_op jit(solution)/shard_map/all_gather | solution.py:67
  245.8 0.1 copy.140
  245.9 0.1 copy.142
  246.0 0.1 reshape.225
  246.1 0.1 broadcast_compare_fusion
  246.2 0.1 iota_compare_fusion.3
  246.2 0.1 reshape.217
  246.3 0.2 fusion.51
  246.5 98.2 %all-reduce.1 = (f32[8]{0:T(128)S(1)}, f32[8,1024]{1,0:T(8,128)S(1)}) all-reduce(f32[8]{0:T(128)S(1)} %reshape.217, f32[8,1024]{1,0:T(8,128)S(1)} %fusion.51), channel_id=1, replica_groups=mesh['dp'=32,'tensor'=16] {'tensor'}, use_global_device_ids=true, to_apply=%region_3.5 | all-reduce | flops 8200 | bytes 65600 | tf_op jit(solution)/shard_map/psum | solution.py:84
  344.7 0.1 multiply_convert_fusion
  344.7 4.2 %all-reduce.6.cloned.1.call-done = (f32[8,2048]{1,0:T(8,128)}, f32[512,1820]{0,1:T(8,128)}) async-done(((f32[8,2048]{1,0:T(8,128)}, f32[512,1820]{0,1:T(8,128)}), (f32[8,2048]{1,0:T(8,128)}, f32[512,1820]{0,1:T(8,128)})) %all-reduce.6.cloned.1.call-update) | async-done | bytes 3792912 | tf_op jit(solution)/shard_map/psum | solution.py:84
  349.0 0.8 multiply_convert_fusion.1
  349.7 1.0 fusion.48
  350.7 0.1 fusion.49
  350.8 0.2 fusion.24
  351.0 1.2 fusion.10
  352.3 0.7 copy.145
  353.0 1.3 fusion.8
  354.2 0.7 copy.146
  355.0 0.9 fusion.14
  355.9 0.8 fusion.5
  (31 shorter events, 0.3 us)
Async XLA Ops:
  7.2 56.0 %copy-start = (bf16[512,2,448]{0,2,1:T(8,128)(2,1)S(1)}, bf16[512,2,448]{0,2,1:T(8,128)(2,1)}, u32[]{:S(2)}) copy-start(bf16[512,2,448]{0,2,1:T(8,128)(2,1)} %param.26) | copy-start | bytes 2752516
  8.6 60.6 %all-to-all-start = ((s32[32,2,4]{2,1,0:T(2,128)}), s32[32,2,4]{2,1,0:T(2,128)S(1)}, u32[]{:S(2)}, u32[]{:S(2)}) async-start(s32[32,2,4]{2,1,0:T(2,128)} %stack.2), calls=%async_computation | async-start | bytes 65536 | tf_op jit(solution)/shard_map/all_to_all | solution.py:65
  22.3 326.7 %all-reduce.6.cloned.1.call-start = ((), (), s32[]{:S(2)}) async-start(), calls=%async_computation.1 | async-start | bytes 7602176 | tf_op jit(solution)/shard_map/psum | solution.py:84
  63.9 2.3 copy-start.1
  66.1 1.0 copy-start.6
  67.1 118.4 %copy-start.2 = (bf16[224,2048]{1,0:T(8,128)(2,1)S(1)}, bf16[224,2048]{1,0:T(8,128)(2,1)}, u32[]{:S(2)}) copy-start(bf16[224,2048]{1,0:T(8,128)(2,1)} %param.20) | copy-start | bytes 2752516
  186.4 0.7 copy-start.4
  186.4 30.0 %copy-start.5 = (s32[1,4]{1,0:T(1,128)S(1)}, s32[1,4]{1,0:T(1,128)}, u32[]{:S(2)}) copy-start(s32[1,4]{1,0:T(1,128)} %param.28) | copy-start | bytes 52
  186.4 59.8 %copy-start.7 = (s32[2]{0:T(128)S(1)}, s32[2]{0:T(128)}, u32[]{:S(2)}) copy-start(s32[2]{0:T(128)} %param.24) | copy-start | bytes 28
  186.4 60.0 %copy-start.3 = (bf16[224,1024]{1,0:T(8,128)(2,1)S(1)}, bf16[224,1024]{1,0:T(8,128)(2,1)}, u32[]{:S(2)}) copy-start(bf16[224,1024]{1,0:T(8,128)(2,1)} %param.21) | copy-start | bytes 1376260
Sparse Core Ops, SparseCore 0:
  186.5 162.3 all-reduce.5
